TPU v7x, 32 devices: a whole 2x2x4 slice. The times are simulated.
32 devices in a mesh: tm: 16 (over z, y, x), tensor: 2 (over core).
Axes of the slice: x: 2, y: 2, z: 4, core: 2. Of those that a mesh axis runs over, the one named last changes fastest.
Arguments:
- noise_start: float32 [1, 16384], replicated, may hold values from -6 to 6
- timesteps: int32 [17], replicated, may hold values from 0 to 599, as said below
- class_labels: int32 [16, 1], P('tm'), may hold values from 0 to 999
- mixing: float32 [2, 16], P(None, 'tm'), may hold values from -0.5 to 0.5
- class_table: bfloat16 [1000, 768], replicated, may hold values from -3 to 3
- time_in: bfloat16 [256, 768], replicated, may hold values from -0.75 to 0.75
- time_out: bfloat16 [768, 768], replicated, may hold values from -0.21875 to 0.21875
- ada_weight: bfloat16 [768, 4608], replicated, may hold values from -0.21875 to 0.21875
- final_ada: bfloat16 [768, 1536], replicated, may hold values from -0.21875 to 0.21875
- patch_weight: bfloat16 [16, 768], replicated, may hold values from -1.5 to 1.5
- q_weight: bfloat16 [768, 768], replicated, may hold values from -1.5 to 1.5
- kv_weight: bfloat16 [768, 1536], replicated, may hold values from -1.5 to 1.5
- out_weight: bfloat16 [768, 768], replicated, may hold values from -0.4375 to 0.4375
- up_weight: bfloat16 [768, 3072], P(None, 'tensor'), may hold values from -0.21875 to 0.21875
- down_weight: bfloat16 [3072, 768], P('tensor'), may hold values from -0.21875 to 0.21875
- final_weight: bfloat16 [768, 16], replicated, may hold values from -0.21875 to 0.21875
Outputs:
- states: float32 [16, 1, 16384], P('tm')
- residuals: float32 [2, 16], P(None, 'tm')
Inputs may be any that keep to these rules, and one draw needn't show every extreme that they name: `timesteps`: strictly decreasing; the first is 599, the last is 0, all others lie from 100 to 549.
All inputs are finite; a program needn't handle non-finite values.
Results may differ from a plain program's by a relative error of at most 0.008.
Values may be sent and summed in bfloat16 or wider, within the bound.
A program may use at most 128 MiB of HBM per device.

v0:
```python
import math
import jax
import jax.numpy as jnp
from jax import lax
from jax.sharding import PartitionSpec as P

D = 768
HEADS = 12
SEQ = 1024
PATCH = 16
CLASSES = 1000
FREQ = 256
IMG = 1
ITERS = 2
LAT = 16384
norm_eps = 1e-06
plan_steps = 1000


def prefix(array, axis, combine, identity):
    size, here = (lax.axis_size(axis), lax.axis_index(axis))
    everything = lax.all_gather(
        array.astype(jnp.bfloat16 if array.dtype == jnp.float32 else array.dtype), axis
    )
    start = jnp.broadcast_to(jnp.asarray(identity, array.dtype), array.shape)

    def step(k, before):
        reached = k < here
        new = combine(before, everything[k].astype(array.dtype))
        return jnp.where(reached, new, before)

    return lax.fori_loop(0, size, step, start)


def shortened(array):
    return jax.tree.map(lambda a: a.astype(jnp.bfloat16) if a.dtype == jnp.float32 else a, array)


def from_behind(value, axis, steps):
    count = lax.axis_size(axis)
    leading, last = (max(0, -steps), min(count, count - steps))
    return lax.ppermute(value, axis, [(source, source + steps) for source in range(leading, last)])


def log_table():
    levels = jnp.arange(plan_steps, dtype=jnp.float32)
    beta_values = 0.0001 + (0.02 - 0.0001) * levels / (plan_steps - 1)
    return jnp.cumsum(jnp.log(1.0 - beta_values))


def alpha_at(moments):
    matches = moments[:, None] == jnp.arange(plan_steps, dtype=jnp.int32)[None, :]
    return jnp.exp(jnp.sum(jnp.where(matches, log_table()[None, :], 0.0), axis=1))


def time_features(moment):
    half_count = FREQ // 2
    freq_rates = jnp.exp(
        -math.log(10000.0) * jnp.arange(half_count, dtype=jnp.float32) / half_count
    )
    angles = moment.astype(jnp.float32) * freq_rates
    return jnp.concatenate([jnp.cos(angles), jnp.sin(angles)])[None, :]


def positions():
    half_width = D // 2
    places = jnp.arange(SEQ, dtype=jnp.float32)[:, None]
    freq_rates = jnp.exp(
        -math.log(10000.0) * jnp.arange(half_width, dtype=jnp.float32) / half_width
    )
    angles = places * freq_rates[None, :]
    return jnp.concatenate([jnp.sin(angles), jnp.cos(angles)], axis=1)


def layer_norm(values):
    center = values - jnp.mean(values, axis=-1, keepdims=True)
    spread = jnp.mean(center * center, axis=-1, keepdims=True)
    return center * lax.rsqrt(spread + norm_eps)


def modulate(values, shift, scale):
    return layer_norm(values) * (1.0 + scale) + shift


def split_rows(matrix, count):
    return [matrix[:, None, column * D : (column + 1) * D] for column in range(count)]


def add_fields(earlier, later_part):
    return earlier + later_part


def pick_entry(vector, wanted):
    matches = jnp.arange(vector.shape[0], dtype=jnp.int32) == wanted
    return jnp.sum(jnp.where(matches, vector, 0))


def per_device(
    noise_start,
    timesteps,
    class_labels,
    mixing,
    class_table,
    time_in,
    time_out,
    ada_weight,
    final_ada,
    patch_weight,
    q_weight,
    kv_weight,
    out_weight,
    up_weight,
    down_weight,
    final_weight,
):
    window_point = lax.axis_index("tm")
    group_size = lax.axis_size("tensor")
    member = lax.axis_index("tensor")
    rows_own = SEQ // group_size
    offset = member * rows_own
    head_dim = D // HEADS
    moment_now = pick_entry(timesteps, window_point)
    moment_next = pick_entry(timesteps, window_point + 1)
    alphas = alpha_at(jnp.stack([moment_now, moment_next]))
    keep_coef = jnp.sqrt(alphas[1] / alphas[0])
    noise_coef = jnp.sqrt(1.0 - alphas[1]) - jnp.sqrt(alphas[1] * (1.0 - alphas[0]) / alphas[0])
    features = time_features(moment_now).astype(jnp.bfloat16)
    time_hidden = jax.nn.silu(
        jnp.dot(features, time_in, preferred_element_type=jnp.float32)
    ).astype(jnp.bfloat16)
    time_embed = jnp.dot(time_hidden, time_out, preferred_element_type=jnp.float32)
    onehot = (class_labels[0][:, None] == jnp.arange(CLASSES, dtype=jnp.int32)[None, :]).astype(
        jnp.bfloat16
    )
    classes = jnp.dot(onehot, class_table, preferred_element_type=jnp.float32)
    summed = jax.nn.silu(time_embed + classes).astype(jnp.bfloat16)
    modul = jnp.dot(summed, ada_weight, preferred_element_type=jnp.float32)
    final_mod = jnp.dot(summed, final_ada, preferred_element_type=jnp.float32)
    shift_attn, scale_attn, gate_attn, shift_mlp, scale_mlp, gate_mlp = split_rows(modul, 6)
    shift_out, scale_out = split_rows(final_mod, 2)
    place_rows = lax.dynamic_slice_in_dim(positions(), offset, rows_own, 0)
    state_in = noise_start
    state_out = noise_start
    previous = noise_start
    residual_rows = []
    for iteration in range(ITERS):
        tokens = state_in.astype(jnp.bfloat16).reshape(IMG, SEQ, PATCH)
        own_tokens = lax.dynamic_slice_in_dim(tokens, offset, rows_own, 1).reshape(
            IMG * rows_own, PATCH
        )
        hidden = jnp.dot(own_tokens, patch_weight, preferred_element_type=jnp.float32).reshape(
            IMG, rows_own, D
        )
        hidden = hidden + place_rows[None]
        attn_in = (
            modulate(hidden, shift_attn, scale_attn).astype(jnp.bfloat16).reshape(IMG * rows_own, D)
        )
        queries = jnp.dot(attn_in, q_weight, preferred_element_type=jnp.float32).astype(
            jnp.bfloat16
        )
        queries = queries.reshape(IMG, rows_own, HEADS, head_dim)
        key_value = jnp.dot(attn_in, kv_weight, preferred_element_type=jnp.float32).astype(
            jnp.bfloat16
        )
        key_value = key_value.reshape(IMG, rows_own, 2 * D)
        gathered = lax.all_gather(key_value, "tensor", axis=1, tiled=True)
        key_heads = gathered[:, :, :D].reshape(IMG, SEQ, HEADS, head_dim)
        value_heads = gathered[:, :, D:].reshape(IMG, SEQ, HEADS, head_dim)
        scores = jnp.einsum(
            "bqhd,bkhd->bhqk", queries, key_heads, preferred_element_type=jnp.float32
        )
        scores = scores * (1.0 / math.sqrt(head_dim))
        attention = jax.nn.softmax(scores, axis=-1).astype(jnp.bfloat16)
        attended = jnp.einsum(
            "bhqk,bkhd->bqhd", attention, value_heads, preferred_element_type=jnp.float32
        )
        attended = attended.astype(jnp.bfloat16).reshape(IMG * rows_own, D)
        projected = jnp.dot(attended, out_weight, preferred_element_type=jnp.float32).reshape(
            IMG, rows_own, D
        )
        hidden = hidden + gate_attn * projected
        stream = lax.all_gather(hidden.astype(jnp.bfloat16), "tensor", axis=1, tiled=True).astype(
            hidden.dtype
        )
        predict_mlp_in = modulate(stream, shift_mlp, scale_mlp).astype(jnp.bfloat16)
        flat_in = predict_mlp_in.reshape(IMG * SEQ, D)
        lifted = jax.nn.gelu(
            jnp.dot(flat_in, up_weight, preferred_element_type=jnp.float32), approximate=True
        )
        lifted = lifted.astype(jnp.bfloat16)
        mlp_sum = lax.psum(
            jnp.dot(lifted, down_weight, preferred_element_type=jnp.float32)
            .reshape(IMG, SEQ, D)
            .astype(jnp.bfloat16),
            "tensor",
        ).astype(jnp.float32)
        stream_out = stream + gate_mlp * mlp_sum
        final_in = (
            modulate(stream_out, shift_out, scale_out).astype(jnp.bfloat16).reshape(IMG * SEQ, D)
        )
        predicted = jnp.dot(final_in, final_weight, preferred_element_type=jnp.float32).reshape(
            IMG, LAT
        )
        drift_now = (keep_coef - 1.0) * state_in + noise_coef * predicted
        slice_width = LAT // group_size
        drift_piece = lax.dynamic_slice_in_dim(drift_now, member * slice_width, slice_width, 1)
        before_piece = prefix(drift_piece, "tm", add_fields, jnp.zeros_like(drift_piece))
        reached = lax.all_gather(
            shortened(before_piece + drift_piece), "tensor", axis=1, tiled=True
        )
        picard_map = noise_start + reached
        residual_rows.append(jnp.mean(jnp.square(picard_map - state_out)))
        state_new = picard_map + mixing[iteration, 0] * (picard_map - previous)
        previous = picard_map
        state_out = state_new
        if iteration + 1 < ITERS:
            state_in = noise_start + from_behind(shortened(state_new - noise_start), "tm", 1)
    return (state_out[None], jnp.stack(residual_rows)[:, None])


def solution(mesh):
    in_specs = (
        P(),
        P(),
        P("tm", None),
        P(None, "tm"),
        P(),
        P(),
        P(),
        P(),
        P(),
        P(),
        P(),
        P(),
        P(),
        P(None, "tensor"),
        P("tensor", None),
        P(),
    )
    out_specs = (P("tm", None, None), P(None, "tm"))
    return jax.shard_map(
        per_device, mesh=mesh, in_specs=in_specs, out_specs=out_specs, check_vma=False
    )
```

profile of v0, /device:TPU:0, one launch (start us, length us, event | category | flops | bytes accessed | tf_op | source)
XLA Modules:
  0.0 339.4 jit_solution(7551914350179567751)
XLA Ops:
  7.3 6.6 %fusion.78 = (f32[1024,384]{1,0:T(8,128)}, f32[1024,384]{1,0:T(8,128)}) fusion(f32[384]{0:T(512)S(1)} %multiply_exponential_fusion), kind=kLoop, calls=%fused_computation.95 | loop fusion | flops 393216 | bytes 3147264 | tf_op jit(solution)/shard_map/sin | solution.py:72
  14.3 1.8 fusion.131
  16.2 1.2 copy-done.6
  20.0 1.6 convolution_reduce_fusion.2
  21.6 1.7 convolution_reduce_fusion.1
  23.3 4.1 %fusion.135 = f32[1,4608]{1,0:T(1,128)S(1)} fusion(bf16[768,1]{0,1:T(2,128)(2,1)S(1)} %reshape.487, bf16[768,4608]{1,0:T(8,128)(2,1)} %param.27), kind=kOutput, calls=%fused_computation.196 | convolution fusion | flops 7077888 | bytes 7097856 | tf_op jit(solution)/shard_map/dot_general | solution.py:137
  27.6 2.7 convolution_convert_fusion.1
  30.6 3.6 %convolution_convert_fusion.3 = bf16[512,768]{1,0:T(8,128)(2,1)} fusion(bf16[768,768]{1,0:T(8,128)(2,1)} %param.30, f32[512,768]{1,0:T(8,128)} %copy-done.6, f32[768]{0:T(1024)S(1)} %get-tuple-element.196, f32[768]{0:T(1024)S(1)} %get-tuple-element.197, f32[512]{0:T(512)S(1)} %add_rsqrt_fusion.5, f32[512]{0:T(512)S(1)} %broadcast_multiply_fusion.5), kind=kOutput, calls=%fused_computation.105 | convolution fusion | flops 606339072 | bytes 3549184 | tf_op jit(solution)/shard_map/dot_general | solution.py:158
  34.2 2.3 copy.41
  36.5 8.7 %all-gather.13.cloned.1.call-done = bf16[1024,1536]{1,0:T(8,128)(2,1)} async-done(((bf16[512,1536]{1,0:T(8,128)(2,1)}), bf16[1024,1536]{1,0:T(8,128)(2,1)}) %all-gather.13.cloned.1.call-update) | async-done | bytes 3145744 | tf_op jit(solution)/shard_map/all_gather | solution.py:166
  45.2 3.8 %fusion.128 = (bf16[1,1024,768]{2,1,0:T(8,128)(2,1)}, bf16[1,1024,768]{2,1,0:T(8,128)(2,1)}) fusion(bf16[1,1024,1536]{2,1,0:T(8,128)(2,1)} %bitcast.198), kind=kLoop, calls=%fused_computation.189 | loop fusion | bytes 6291456 | tf_op jit(solution)/shard_map/slice | solution.py:167
  49.0 2.6 copy.42
  51.6 2.6 copy.40
  54.2 13.0 %fusion.132 = (f32[12,512]{1,0:T(8,128)S(1)}, f32[12,512,1024]{2,1,0:T(8,128)}) fusion(bf16[512,12,64]{0,2,1:T(8,128)(2,1)} %bitcast.203, bf16[1024,12,64]{0,2,1:T(8,128)(2,1)} %bitcast.199), kind=kOutput, calls=%fused_computation.193 | convolution fusion | flops 824181760 | bytes 27549696 | tf_op jit(solution)/shard_map/sub | solution.py:173
  67.2 10.9 %fusion.90 = bf16[12,64,512]{2,1,0:T(8,128)(2,1)S(1)} fusion(bf16[1024,12,64]{0,2,1:T(8,128)(2,1)} %bitcast.200, f32[12,512,1024]{2,1,0:T(8,128)} %get-tuple-element.240, f32[12,512]{1,0:T(8,128)S(1)} %get-tuple-element.239), kind=kOutput, calls=%fused_computation.103 | convolution fusion | flops 818282496 | bytes 27549696 | tf_op jit(solution)/shard_map/bhqk,bkhd->bqhd/dot_general | solution.py:174
  78.1 1.7 add_convert_fusion.4
  80.5 10.6 %all-gather.15.cloned.1.call-done = bf16[1024,768]{1,0:T(8,128)(2,1)} async-done(((bf16[512,768]{1,0:T(8,128)(2,1)}), bf16[1024,768]{1,0:T(8,128)(2,1)}) %all-gather.15.cloned.1.call-update) | async-done | bytes 1572880 | tf_op jit(solution)/shard_map/all_gather | solution.py:182
  91.0 1.8 convert_reduce_fusion.1
  93.6 9.4 %fusion.86 = bf16[1,1024,768]{2,1,0:T(8,128)(2,1)} fusion(bf16[1536,768]{1,0:T(8,128)(2,1)} %param.34, bf16[768,1536]{1,0:T(8,128)(2,1)} %param.33, bf16[1024,768]{1,0:T(8,128)(2,1)} %all-gather.15.cloned.1.call-done, f32[768]{0:T(1024)S(1)} %get-tuple-element.199, f32[768]{0:T(1024)S(1)} %get-tuple-element.195, f32[1024]{0:T(1024)S(1)} %add_rsqrt_fusion.3, ...), kind=kOutput, calls=%fused_computation.99 | convolution fusion | flops 4851499008 | bytes 7878656 | tf_op jit(solution)/shard_map/dot_general | solution.py:192
  103.5 1.4 pad_add_fusion
  110.2 2.1 fusion.136
  112.4 12.3 %all-reduce.4.cloned.1.call-done = bf16[1,1024,768]{2,1,0:T(8,128)(2,1)} async-done(((bf16[1,1024,768]{2,1,0:T(8,128)(2,1)}), bf16[1,1024,768]{2,1,0:T(8,128)(2,1)}) %all-reduce.4.cloned.1.call-update) | async-done | bytes 1572880 | tf_op jit(solution)/shard_map/psum | solution.py:191
  124.7 2.6 fusion.59
  128.4 1.1 fusion.99
  130.0 44.0 %all-gather.6 = bf16[16,1,8192]{2,1,0:T(2,128)(2,1)S(1)} all-gather(bf16[1,1,8192]{2,1,0:T(2,128)(2,1)S(1)} %get-tuple-element.224), channel_id=4, replica_groups=mesh['tm'=16,'tensor'=2] {'tm'}, dimensions={0}, use_global_device_ids=true | all-gather | bytes 278528 | tf_op jit(solution)/shard_map/all_gather | solution.py:22
  174.0 1.3 while.28
  175.4 1.9 all_gather.34
  177.9 1.3 collective-permute-start
  179.2 1.9 collective-permute-done
  181.6 1.8 fusion.133
  184.6 2.7 convolution_convert_fusion
  187.5 2.7 convolution_convert_fusion.2
  190.5 7.5 %all-gather.17.cloned.1.call-done = bf16[1024,1536]{1,0:T(8,128)(2,1)} async-done(((bf16[512,1536]{1,0:T(8,128)(2,1)}), bf16[1024,1536]{1,0:T(8,128)(2,1)}) %all-gather.17.cloned.1.call-update) | async-done | bytes 3145744 | tf_op jit(solution)/shard_map/all_gather | solution.py:166
  198.0 3.2 fusion.127
  201.2 2.6 copy.46
  203.8 1.6 copy.44
  205.4 12.9 %fusion.134 = (f32[12,512]{1,0:T(8,128)S(1)}, f32[12,512,1024]{2,1,0:T(8,128)}) fusion(bf16[512,12,64]{0,2,1:T(8,128)(2,1)S(1)} %bitcast.204, bf16[1024,12,64]{0,2,1:T(8,128)(2,1)} %bitcast.201), kind=kOutput, calls=%fused_computation.195 | convolution fusion | flops 824181760 | bytes 27549696 | tf_op jit(solution)/shard_map/sub | solution.py:173
  218.3 10.9 %fusion.89 = bf16[12,64,512]{2,1,0:T(8,128)(2,1)S(1)} fusion(bf16[1024,12,64]{0,2,1:T(8,128)(2,1)} %bitcast.202, f32[12,512,1024]{2,1,0:T(8,128)} %get-tuple-element.244, f32[12,512]{1,0:T(8,128)S(1)} %get-tuple-element.243), kind=kOutput, calls=%fused_computation.102 | convolution fusion | flops 818282496 | bytes 27549696 | tf_op jit(solution)/shard_map/bhqk,bkhd->bqhd/dot_general | solution.py:174
  229.3 1.7 add_convert_fusion.2
  231.3 10.9 %all-gather.19.cloned.1.call-done = bf16[1024,768]{1,0:T(8,128)(2,1)} async-done(((bf16[512,768]{1,0:T(8,128)(2,1)}), bf16[1024,768]{1,0:T(8,128)(2,1)}) %all-gather.19.cloned.1.call-update) | async-done | bytes 1572880 | tf_op jit(solution)/shard_map/all_gather | solution.py:182
  242.1 1.8 convert_reduce_fusion
  244.6 8.9 %fusion.83 = bf16[1,1024,768]{2,1,0:T(8,128)(2,1)} fusion(bf16[1536,768]{1,0:T(8,128)(2,1)} %param.34, bf16[768,1536]{1,0:T(8,128)(2,1)} %param.33, bf16[1024,768]{1,0:T(8,128)(2,1)S(1)} %copy-done.4, f32[1024]{0:T(1024)S(1)} %add_rsqrt_fusion.1, f32[1024]{0:T(1024)S(1)} %broadcast_multiply_fusion.1, f32[768]{0:T(1024)S(1)} %get-tuple-element.199, ...), kind=kOutput, calls=%fused_computation.98 | convolution fusion | flops 4851499008 | bytes 7878656 | tf_op jit(solution)/shard_map/dot_general | solution.py:192
  253.6 21.7 %all-reduce.6.cloned.1.call-done = bf16[1,1024,768]{2,1,0:T(8,128)(2,1)} async-done(((bf16[1,1024,768]{2,1,0:T(8,128)(2,1)}), bf16[1,1024,768]{2,1,0:T(8,128)(2,1)}) %all-reduce.6.cloned.1.call-update) | async-done | bytes 1572880 | tf_op jit(solution)/shard_map/psum | solution.py:191
  275.3 2.1 fusion.58
  280.4 44.0 %all-gather.7 = bf16[16,1,8192]{2,1,0:T(2,128)(2,1)S(1)} all-gather(bf16[1,1,8192]{2,1,0:T(2,128)(2,1)S(1)} %get-tuple-element.220), channel_id=7, replica_groups=mesh['tm'=16,'tensor'=2] {'tm'}, dimensions={0}, use_global_device_ids=true | all-gather | bytes 278528 | tf_op jit(solution)/shard_map/all_gather | solution.py:22
  324.4 1.3 while.29
  325.8 1.9 all_gather.39
  327.6 2.7 multiply_reduce_fusion.7
  (146 shorter events, 16.5 us)
Async XLA Ops:
  7.2 20.4 %copy-start = (bf16[768,1536]{1,0:T(8,128)(2,1)S(1)}, bf16[768,1536]{1,0:T(8,128)(2,1)}, u32[]{:S(2)}) copy-start(bf16[768,1536]{1,0:T(8,128)(2,1)} %param.31) | copy-start | bytes 7077892
  7.2 6.7 %copy-start.13 = (f32[1,16384]{1,0:T(1,128)S(1)}, f32[1,16384]{1,0:T(1,128)}, u32[]{:S(2)}) copy-start(f32[1,16384]{1,0:T(1,128)} %param.20) | copy-start | bytes 196612
  7.2 7.1 %copy-start.15 = (bf16[16,768]{1,0:T(8,128)(2,1)S(1)}, bf16[16,768]{1,0:T(8,128)(2,1)}, u32[]{:S(2)}) copy-start(bf16[16,768]{1,0:T(8,128)(2,1)} %param.29) | copy-start | bytes 73732
  7.2 38.0 %all-gather.13.cloned.1.call-start = ((), (), s32[]{:S(2)}) async-start(), calls=%async_computation.2 | async-start | bytes 4718592 | tf_op jit(solution)/shard_map/all_gather | solution.py:166
  14.3 3.4 copy-start.17
  14.3 4.8 %copy-start.14 = (bf16[256,768]{1,0:T(8,128)(2,1)S(1)}, bf16[256,768]{1,0:T(8,128)(2,1)}, u32[]{:S(2)}) copy-start(bf16[256,768]{1,0:T(8,128)(2,1)} %param.25) | copy-start | bytes 1179652
  16.2 1.2 copy-start.6
  23.3 4.2 %copy-start.7 = (f32[512,768]{1,0:T(8,128)S(1)}, f32[512,768]{1,0:T(8,128)}, u32[]{:S(2)}) copy-start(f32[512,768]{1,0:T(8,128)} %copy-done.6) | copy-start | bytes 4718596
  30.2 60.8 %all-gather.15.cloned.1.call-start = ((), (), s32[]{:S(2)}) async-start(), calls=%async_computation.3 | async-start | bytes 2359296 | tf_op jit(solution)/shard_map/all_gather | solution.py:182
  67.2 10.9 %copy-start.8 = (f32[512,768]{1,0:T(8,128)S(1)}, f32[512,768]{1,0:T(8,128)}, u32[]{:S(2)}) copy-start(f32[512,768]{1,0:T(8,128)} %copy-done.6) | copy-start | bytes 4718596
  67.2 10.9 %copy-start.18 = (bf16[768,768]{1,0:T(8,128)(2,1)S(1)}, bf16[768,768]{1,0:T(8,128)(2,1)}, u32[]{:S(2)}) copy-start(bf16[768,768]{1,0:T(8,128)(2,1)} %param.32) | copy-start | bytes 3538948
  79.9 44.8 %all-reduce.4.cloned.1.call-start = ((), (), s32[]{:S(2)}) async-start(), calls=%async_computation | async-start | bytes 3145728 | tf_op jit(solution)/shard_map/psum | solution.py:191
  91.0 1.9 copy-start.2
  93.5 16.1 %copy-start.16 = (f32[2,1]{0,1:T(1,128)S(1)}, f32[2,1]{0,1:T(1,128)}, u32[]{:S(2)}) copy-start(f32[2,1]{0,1:T(1,128)} %param.23) | copy-start | bytes 28
  103.0 95.0 %all-gather.17.cloned.1.call-start = ((), (), s32[]{:S(2)}) async-start(), calls=%async_computation.4 | async-start | bytes 4718592 | tf_op jit(solution)/shard_map/all_gather | solution.py:166
  124.7 2.6 copy-start.3
  124.7 2.8 copy-start.9
  127.3 1.1 copy-start.20
  177.9 3.2 collective-permute-start
  183.4 1.2 copy-start.10
  187.3 54.8 %all-gather.19.cloned.1.call-start = ((), (), s32[]{:S(2)}) async-start(), calls=%async_computation.5 | async-start | bytes 2359296 | tf_op jit(solution)/shard_map/all_gather | solution.py:182
  218.3 10.9 %copy-start.11 = (f32[512,768]{1,0:T(8,128)S(1)}, f32[512,768]{1,0:T(8,128)}, u32[]{:S(2)}) copy-start(f32[512,768]{1,0:T(8,128)} %copy-done.10) | copy-start | bytes 4718596
  218.3 10.9 %copy-start.19 = (bf16[768,768]{1,0:T(8,128)(2,1)S(1)}, bf16[768,768]{1,0:T(8,128)(2,1)}, u32[]{:S(2)}) copy-start(bf16[768,768]{1,0:T(8,128)(2,1)} %param.32) | copy-start | bytes 3538948
  231.0 44.3 %all-reduce.6.cloned.1.call-start = ((), (), s32[]{:S(2)}) async-start(), calls=%async_computation.1 | async-start | bytes 3145728 | tf_op jit(solution)/shard_map/psum | solution.py:191
  242.1 1.9 copy-start.4
  275.3 2.1 copy-start.12
  277.4 1.4 copy-start.5
  278.8 53.5 %copy-start.1 = (bf16[768,1536]{1,0:T(8,128)(2,1)S(1)}, bf16[768,1536]{1,0:T(8,128)(2,1)}, u32[]{:S(2)}) copy-start(bf16[768,1536]{1,0:T(8,128)(2,1)} %param.31) | copy-start | bytes 7077892
Sparse Core Ops, SparseCore 0:
  30.4 14.8 all-gather.12
  80.0 10.9 all-gather.14
  103.1 21.5 all-reduce.3
  187.4 10.4 all-gather.16
  231.1 10.9 all-gather.18
  253.7 21.5 all-reduce.5
where the time goes:
time: 344 us; the launch traced here: 339 us
  matrix products  96.6 us (28%)
  blocking collectives  91.7 us (27%)
  waiting for transfers between devices  73.7 us (21%)
  other arithmetic  27.8 us (8%)
  local copies, waits for them, and re-layouts  24.7 us (7%)
  between operations  21.3 us (6%)
    all_gather x2, blocking collectives, prefix(): lax.all_gather(array.astype(jnp.bfloat16 if array.dtype == jnp.float32 el...  88 us
    psum x2, waiting for transfers between devices, per_device(): lax.psum(jnp.dot(lifted, down_weight, preferred_element_type=jnp.float32)...  34 us
    sub x2, matrix products, per_device(): attention = jax.nn.softmax(scores, axis=-1).astype(jnp.bfloat16)  25.9 us
    dot_general x2, matrix products, per_device(): jnp.einsum('bhqk,bkhd->bqhd', attention, value_heads, preferred_element_t...  21.8 us
    all_gather x2, waiting for transfers between devices, per_device(): lax.all_gather(hidden.astype(jnp.bfloat16), 'tensor', axis=1, tiled=True)  21.4 us
    dot_general x2, matrix products, per_device(): jnp.dot(lifted, down_weight, preferred_element_type=jnp.float32)  18.3 us
    all_gather x2, waiting for transfers between devices, per_device(): gathered = lax.all_gather(key_value, 'tensor', axis=1, tiled=True)  16.2 us
    slice x4, local copies, waits for them, and re-layouts, per_device(): key_heads = gathered[:, :, :D].reshape(IMG, SEQ, HEADS, head_dim)  12.2 us
  transfers between devices with their start and end apart: 7, of which 7 were waited for; matrix products, arithmetic and copies ran while one was open for 4% of the time, Pallas kernels for 0%

commit v1 on v0

--- a/solution.py
+++ b/solution.py
@@ -179,9 +179,20 @@
             IMG, rows_own, D
         )
         hidden = hidden + gate_attn * projected
-        stream = lax.all_gather(hidden.astype(jnp.bfloat16), "tensor", axis=1, tiled=True).astype(
-            hidden.dtype
-        )
+
+        def _choose_threads(sample):
+            found_now = jnp.concatenate(
+                lax.all_to_all(
+                    jnp.stack([sample for _ in range(lax.axis_size("tensor"))]),
+                    axis_name="tensor",
+                    split_axis=0,
+                    concat_axis=0,
+                ),
+                axis=1,
+            )
+            return found_now
+
+        stream = _choose_threads(hidden.astype(jnp.bfloat16)).astype(hidden.dtype)
         predict_mlp_in = modulate(stream, shift_mlp, scale_mlp).astype(jnp.bfloat16)
         flat_in = predict_mlp_in.reshape(IMG * SEQ, D)
         lifted = jax.nn.gelu(

time: 344 us -> 336 us (0.977)
  waiting for transfers between devices: 73.7 us -> 52.2 us
  blocking collectives: 91.7 us -> 102 us
  other arithmetic: 27.8 us -> 32.9 us
    all_gather x2 -> x0, waiting for transfers between devices: 21.4 us -> none  [per_device(): lax.all_gather(hidden.astype(jnp.bfloat16), 'tensor', axis=1, tiled=True)]
    all_to_all x0 -> x2, blocking collectives: none -> 10.7 us  [_choose_threads(): lax.all_to_all(jnp.stack([sample for _ in range(lax.axis_size('tensor'))]...]
    convert_element_type x0 -> x2, other arithmetic: none -> 3.55 us  [per_device(): predict_mlp_in = modulate(stream, shift_mlp, scale_mlp).astype(jnp.bfloat16)]
  transfers between devices with their start and end apart: 7 -> 5, of which waited for: 7 -> 5; matrix products, arithmetic and copies ran while one was open for 4% -> 4% of each run, Pallas kernels for 0% -> 0%
where the time goes in v1:
time: 336 us; the launch traced here: 331 us
  blocking collectives  102 us (30%)
  matrix products  94.9 us (28%)
  waiting for transfers between devices  52.2 us (16%)
  other arithmetic  32.9 us (10%)
  local copies, waits for them, and re-layouts  25.4 us (8%)
  between operations  21 us (6%)
    all_gather x2, blocking collectives, prefix(): lax.all_gather(array.astype(jnp.bfloat16 if array.dtype == jnp.float32 el...  88 us
    psum x2, waiting for transfers between devices, per_device(): lax.psum(jnp.dot(lifted, down_weight, preferred_element_type=jnp.float32)...  34 us
    sub x2, matrix products, per_device(): attention = jax.nn.softmax(scores, axis=-1).astype(jnp.bfloat16)  25.9 us
    dot_general x2, matrix products, per_device(): jnp.einsum('bhqk,bkhd->bqhd', attention, value_heads, preferred_element_t...  21.8 us
    dot_general x2, matrix products, per_device(): jnp.dot(lifted, down_weight, preferred_element_type=jnp.float32)  18.6 us
    all_gather x2, waiting for transfers between devices, per_device(): gathered = lax.all_gather(key_value, 'tensor', axis=1, tiled=True)  16.2 us
    slice x4, local copies, waits for them, and re-layouts, per_device(): key_heads = gathered[:, :, :D].reshape(IMG, SEQ, HEADS, head_dim)  12.2 us
    all_to_all x2, blocking collectives, _choose_threads(): lax.all_to_all(jnp.stack([sample for _ in range(lax.axis_size('tensor'))]...  10.7 us
  transfers between devices with their start and end apart: 5, of which 5 were waited for; matrix products, arithmetic and copies ran while one was open for 4% of the time, Pallas kernels for 0%

profile of v1, /device:TPU:0, one launch (start us, length us, event | category | flops | bytes accessed | tf_op | source)
XLA Modules:
  0.0 331.5 jit_solution(14280559630135858034)
XLA Ops:
  7.3 6.6 %fusion.54 = (f32[1024,384]{1,0:T(8,128)}, f32[1024,384]{1,0:T(8,128)}) fusion(f32[384]{0:T(512)S(1)} %multiply_exponential_fusion), kind=kLoop, calls=%fused_computation.77 | loop fusion | flops 393216 | bytes 3147264 | tf_op jit(solution)/shard_map/sin | solution.py:72
  14.3 1.8 fusion.103
  16.2 1.2 copy-done.4
  20.0 1.6 convolution_reduce_fusion.2
  21.6 1.7 convolution_reduce_fusion.1
  23.3 4.1 %fusion.111 = f32[1,4608]{1,0:T(1,128)S(1)} fusion(bf16[768,1]{0,1:T(2,128)(2,1)S(1)} %reshape.669, bf16[768,4608]{1,0:T(8,128)(2,1)} %param.27), kind=kOutput, calls=%fused_computation.186 | convolution fusion | flops 7077888 | bytes 7097856 | tf_op jit(solution)/shard_map/dot_general | solution.py:137
  27.6 2.7 convolution_convert_fusion.1
  30.6 3.6 %convolution_convert_fusion.3 = bf16[512,768]{1,0:T(8,128)(2,1)} fusion(bf16[768,768]{1,0:T(8,128)(2,1)} %param.30, f32[512,768]{1,0:T(8,128)} %copy-done.4, f32[768]{0:T(1024)S(1)} %get-tuple-element.196, f32[768]{0:T(1024)S(1)} %get-tuple-element.197, f32[512]{0:T(512)S(1)} %add_rsqrt_fusion.5, f32[512]{0:T(512)S(1)} %broadcast_multiply_fusion.3), kind=kOutput, calls=%fused_computation.87 | convolution fusion | flops 606339072 | bytes 3549184 | tf_op jit(solution)/shard_map/dot_general | solution.py:158
  34.2 2.3 copy.41
  36.5 8.7 %all-gather.9.cloned.1.call-done = bf16[1024,1536]{1,0:T(8,128)(2,1)} async-done(((bf16[512,1536]{1,0:T(8,128)(2,1)}), bf16[1024,1536]{1,0:T(8,128)(2,1)}) %all-gather.9.cloned.1.call-update) | async-done | bytes 3145744 | tf_op jit(solution)/shard_map/all_gather | solution.py:166
  45.2 3.8 %fusion.100 = (bf16[1,1024,768]{2,1,0:T(8,128)(2,1)}, bf16[1,1024,768]{2,1,0:T(8,128)(2,1)}) fusion(bf16[1,1024,1536]{2,1,0:T(8,128)(2,1)} %bitcast.150), kind=kLoop, calls=%fused_computation.177 | loop fusion | bytes 6291456 | tf_op jit(solution)/shard_map/slice | solution.py:167
  49.0 2.6 copy.42
  51.6 2.6 copy.40
  54.2 13.0 %fusion.104 = (f32[12,512]{1,0:T(8,128)S(1)}, f32[12,512,1024]{2,1,0:T(8,128)}) fusion(bf16[512,12,64]{0,2,1:T(8,128)(2,1)} %bitcast.155, bf16[1024,12,64]{0,2,1:T(8,128)(2,1)} %bitcast.151), kind=kOutput, calls=%fused_computation.181 | convolution fusion | flops 824181760 | bytes 27549696 | tf_op jit(solution)/shard_map/sub | solution.py:173
  67.2 10.9 %fusion.66 = bf16[12,64,512]{2,1,0:T(8,128)(2,1)S(1)} fusion(bf16[1024,12,64]{0,2,1:T(8,128)(2,1)} %bitcast.152, f32[12,512,1024]{2,1,0:T(8,128)} %get-tuple-element.244, f32[12,512]{1,0:T(8,128)S(1)} %get-tuple-element.243), kind=kOutput, calls=%fused_computation.85 | convolution fusion | flops 818282496 | bytes 27549696 | tf_op jit(solution)/shard_map/bhqk,bkhd->bqhd/dot_general | solution.py:174
  79.1 5.5 %all_to_all.10 = bf16[2,1,512,768]{3,2,1,0:T(8,128)(2,1)S(1)} all-to-all(bf16[2,1,512,768]{3,2,1,0:T(8,128)(2,1)S(1)} %pad_maximum_fusion), channel_id=1, replica_groups=mesh['tm'=16,'tensor'=2] {'tensor'}, dimensions={0} | all-to-all | bytes 3145728 | tf_op jit(solution)/shard_map/all_to_all | solution.py:185
  84.9 2.2 multiply_reduce_fusion.5
  87.1 1.8 fusion.35
  88.9 9.3 %fusion.62 = bf16[1,1024,768]{2,1,0:T(8,128)(2,1)} fusion(bf16[1536,768]{1,0:T(8,128)(2,1)} %param.34, bf16[1024,768]{1,0:T(8,128)(2,1)} %fusion.35, bf16[768,1536]{1,0:T(8,128)(2,1)} %param.33), kind=kOutput, calls=%fused_computation.81 | convolution fusion | flops 4846780416 | bytes 7864320 | tf_op jit(solution)/shard_map/dot_general | solution.py:203
  98.7 1.4 pad_add_fusion
  105.5 2.1 fusion.112
  107.7 12.3 %all-reduce.4.cloned.1.call-done = bf16[1,1024,768]{2,1,0:T(8,128)(2,1)} async-done(((bf16[1,1024,768]{2,1,0:T(8,128)(2,1)}), bf16[1,1024,768]{2,1,0:T(8,128)(2,1)}) %all-reduce.4.cloned.1.call-update) | async-done | bytes 1572880 | tf_op jit(solution)/shard_map/psum | solution.py:202
  119.9 3.0 fusion.75
  124.5 1.0 fusion.69
  126.1 44.0 %all-gather.4 = bf16[16,1,8192]{2,1,0:T(2,128)(2,1)S(1)} all-gather(bf16[1,1,8192]{2,1,0:T(2,128)(2,1)S(1)} %get-tuple-element.226), channel_id=3, replica_groups=mesh['tm'=16,'tensor'=2] {'tm'}, dimensions={0}, use_global_device_ids=true | all-gather | bytes 278528 | tf_op jit(solution)/shard_map/all_gather | solution.py:22
  170.1 1.3 while.28
  171.4 1.9 all_gather.27
  174.0 1.3 collective-permute-start
  175.3 1.9 collective-permute-done
  177.6 1.8 fusion.105
  180.7 2.7 convolution_convert_fusion
  183.6 2.7 convolution_convert_fusion.2
  186.5 7.5 %all-gather.11.cloned.1.call-done = bf16[1024,1536]{1,0:T(8,128)(2,1)} async-done(((bf16[512,1536]{1,0:T(8,128)(2,1)}), bf16[1024,1536]{1,0:T(8,128)(2,1)}) %all-gather.11.cloned.1.call-update) | async-done | bytes 3145744 | tf_op jit(solution)/shard_map/all_gather | solution.py:166
  194.0 3.2 fusion.99
  197.2 2.6 copy.46
  199.8 1.6 copy.44
  201.5 12.9 %fusion.106 = (f32[12,512]{1,0:T(8,128)S(1)}, f32[12,512,1024]{2,1,0:T(8,128)}) fusion(bf16[512,12,64]{0,2,1:T(8,128)(2,1)S(1)} %bitcast.156, bf16[1024,12,64]{0,2,1:T(8,128)(2,1)} %bitcast.153), kind=kOutput, calls=%fused_computation.183 | convolution fusion | flops 824181760 | bytes 27549696 | tf_op jit(solution)/shard_map/sub | solution.py:173
  214.4 10.9 %fusion.65 = bf16[12,64,512]{2,1,0:T(8,128)(2,1)S(1)} fusion(bf16[1024,12,64]{0,2,1:T(8,128)(2,1)} %bitcast.154, f32[12,512,1024]{2,1,0:T(8,128)} %get-tuple-element.248, f32[12,512]{1,0:T(8,128)S(1)} %get-tuple-element.247), kind=kOutput, calls=%fused_computation.84 | convolution fusion | flops 818282496 | bytes 27549696 | tf_op jit(solution)/shard_map/bhqk,bkhd->bqhd/dot_general | solution.py:174
  226.3 5.2 %all_to_all.11 = bf16[2,1,512,768]{3,2,1,0:T(8,128)(2,1)S(1)} all-to-all(bf16[2,1,512,768]{3,2,1,0:T(8,128)(2,1)S(1)} %pad_maximum_fusion.1), channel_id=1, replica_groups=mesh['tm'=16,'tensor'=2] {'tensor'}, dimensions={0} | all-to-all | bytes 3145728 | tf_op jit(solution)/shard_map/all_to_all | solution.py:185
  231.8 2.2 multiply_reduce_fusion.3
  233.9 1.8 fusion.31
  235.7 9.3 %fusion.59 = bf16[1,1024,768]{2,1,0:T(8,128)(2,1)} fusion(bf16[1536,768]{1,0:T(8,128)(2,1)} %param.34, bf16[1024,768]{1,0:T(8,128)(2,1)} %fusion.31, bf16[768,1536]{1,0:T(8,128)(2,1)} %param.33), kind=kOutput, calls=%fused_computation.80 | convolution fusion | flops 4846780416 | bytes 7864320 | tf_op jit(solution)/shard_map/dot_general | solution.py:203
  245.0 21.7 %all-reduce.6.cloned.1.call-done = bf16[1,1024,768]{2,1,0:T(8,128)(2,1)} async-done(((bf16[1,1024,768]{2,1,0:T(8,128)(2,1)}), bf16[1,1024,768]{2,1,0:T(8,128)(2,1)}) %all-reduce.6.cloned.1.call-update) | async-done | bytes 1572880 | tf_op jit(solution)/shard_map/psum | solution.py:202
  266.7 3.0 fusion.76
  272.8 44.0 %all-gather.5 = bf16[16,1,8192]{2,1,0:T(2,128)(2,1)S(1)} all-gather(bf16[1,1,8192]{2,1,0:T(2,128)(2,1)S(1)} %get-tuple-element.220), channel_id=5, replica_groups=mesh['tm'=16,'tensor'=2] {'tm'}, dimensions={0}, use_global_device_ids=true | all-gather | bytes 278528 | tf_op jit(solution)/shard_map/all_gather | solution.py:22
  316.9 1.3 while.29
  318.2 1.9 all_gather.31
  320.1 2.7 multiply_reduce_fusion.9
  (144 shorter events, 17.4 us)
Async XLA Ops:
  7.2 20.4 %copy-start = (bf16[768,1536]{1,0:T(8,128)(2,1)S(1)}, bf16[768,1536]{1,0:T(8,128)(2,1)}, u32[]{:S(2)}) copy-start(bf16[768,1536]{1,0:T(8,128)(2,1)} %param.31) | copy-start | bytes 7077892
  7.2 6.7 %copy-start.11 = (f32[1,16384]{1,0:T(1,128)S(1)}, f32[1,16384]{1,0:T(1,128)}, u32[]{:S(2)}) copy-start(f32[1,16384]{1,0:T(1,128)} %param.20) | copy-start | bytes 196612
  7.2 7.1 %copy-start.13 = (bf16[16,768]{1,0:T(8,128)(2,1)S(1)}, bf16[16,768]{1,0:T(8,128)(2,1)}, u32[]{:S(2)}) copy-start(bf16[16,768]{1,0:T(8,128)(2,1)} %param.29) | copy-start | bytes 73732
  7.2 38.0 %all-gather.9.cloned.1.call-start = ((), (), s32[]{:S(2)}) async-start(), calls=%async_computation.4 | async-start | bytes 4718592 | tf_op jit(solution)/shard_map/all_gather | solution.py:166
  14.3 3.4 %copy-start.15 = (s32[17]{0:T(128)S(1)}, s32[17]{0:T(128)}, u32[]{:S(2)}) copy-start(s32[17]{0:T(128)} %param.21) | copy-start | bytes 208
  14.3 4.8 %copy-start.12 = (bf16[256,768]{1,0:T(8,128)(2,1)S(1)}, bf16[256,768]{1,0:T(8,128)(2,1)}, u32[]{:S(2)}) copy-start(bf16[256,768]{1,0:T(8,128)(2,1)} %param.25) | copy-start | bytes 1179652
  16.2 1.2 copy-start.4
  23.3 4.2 %copy-start.5 = (f32[512,768]{1,0:T(8,128)S(1)}, f32[512,768]{1,0:T(8,128)}, u32[]{:S(2)}) copy-start(f32[512,768]{1,0:T(8,128)} %copy-done.4) | copy-start | bytes 4718596
  30.2 89.7 %all-reduce.4.cloned.1.call-start = ((), (), s32[]{:S(2)}) async-start(), calls=%async_computation.2 | async-start | bytes 3145728 | tf_op jit(solution)/shard_map/psum | solution.py:202
  67.2 10.9 %copy-start.6 = (f32[512,768]{1,0:T(8,128)S(1)}, f32[512,768]{1,0:T(8,128)}, u32[]{:S(2)}) copy-start(f32[512,768]{1,0:T(8,128)} %copy-done.4) | copy-start | bytes 4718596
  67.2 10.9 %copy-start.16 = (bf16[768,768]{1,0:T(8,128)(2,1)S(1)}, bf16[768,768]{1,0:T(8,128)(2,1)}, u32[]{:S(2)}) copy-start(bf16[768,768]{1,0:T(8,128)(2,1)} %param.32) | copy-start | bytes 3538948
  88.9 16.0 %copy-start.14 = (f32[2,1]{0,1:T(1,128)S(1)}, f32[2,1]{0,1:T(1,128)}, u32[]{:S(2)}) copy-start(f32[2,1]{0,1:T(1,128)} %param.23) | copy-start | bytes 28
  98.2 95.8 %all-gather.11.cloned.1.call-start = ((), (), s32[]{:S(2)}) async-start(), calls=%async_computation.5 | async-start | bytes 4718592 | tf_op jit(solution)/shard_map/all_gather | solution.py:166
  119.9 3.3 copy-start.2
  119.9 3.8 %copy-start.9 = (bf16[1,1024,768]{2,1,0:T(8,128)(2,1)S(1)}, bf16[1,1024,768]{2,1,0:T(8,128)(2,1)}, u32[]{:S(2)}) copy-start(bf16[1,1024,768]{2,1,0:T(8,128)(2,1)} %all-reduce.4.cloned.1.call-done) | copy-start | bytes 4718596
  123.7 0.8 copy-start.18
  174.0 3.2 collective-permute-start
  179.4 1.2 copy-start.7
  183.4 83.4 %all-reduce.6.cloned.1.call-start = ((), (), s32[]{:S(2)}) async-start(), calls=%async_computation.3 | async-start | bytes 3145728 | tf_op jit(solution)/shard_map/psum | solution.py:202
  214.4 10.9 %copy-start.8 = (f32[512,768]{1,0:T(8,128)S(1)}, f32[512,768]{1,0:T(8,128)}, u32[]{:S(2)}) copy-start(f32[512,768]{1,0:T(8,128)} %copy-done.7) | copy-start | bytes 4718596
  214.4 10.9 %copy-start.17 = (bf16[768,768]{1,0:T(8,128)(2,1)S(1)}, bf16[768,768]{1,0:T(8,128)(2,1)}, u32[]{:S(2)}) copy-start(bf16[768,768]{1,0:T(8,128)(2,1)} %param.32) | copy-start | bytes 3538948
  266.7 3.3 copy-start.3
  266.7 3.8 %copy-start.10 = (bf16[1,1024,768]{2,1,0:T(8,128)(2,1)S(1)}, bf16[1,1024,768]{2,1,0:T(8,128)(2,1)}, u32[]{:S(2)}) copy-start(bf16[1,1024,768]{2,1,0:T(8,128)(2,1)} %all-reduce.6.cloned.1.call-done) | copy-start | bytes 4718596
  271.3 53.4 %copy-start.1 = (bf16[768,1536]{1,0:T(8,128)(2,1)S(1)}, bf16[768,1536]{1,0:T(8,128)(2,1)}, u32[]{:S(2)}) copy-start(bf16[768,1536]{1,0:T(8,128)(2,1)} %param.31) | copy-start | bytes 7077892
Sparse Core Ops, SparseCore 0:
  30.4 14.8 all-gather.8
  98.4 21.5 all-reduce.3
  183.5 10.5 all-gather.10
  245.1 21.5 all-reduce.5
